TPU v7x, 32 devices: a whole 2x2x4 slice. The times are simulated.
32 devices in a mesh: dp: 2 (over core), row: 4 (over y, x), col: 4 (over z).
Axes of the slice: x: 2, y: 2, z: 4, core: 2. Of those that a mesh axis runs over, the one named last changes fastest.
Arguments:
- inputs: bfloat16 [2, 16, 4, 16, 2048], P('dp', 'row', None, None, 'col'), may hold values from -6 to 6
- up_weight: bfloat16 [2048, 4096], P(None, 'col'), may hold values from -0.1875 to 0.1875
- down_weight: bfloat16 [2048, 4096], P(None, 'col'), may hold values from -0.125 to 0.125
- kernel: float32 [125, 4096], P(None, 'col'), may hold values from -0.625 to 0.625
- cotangent: bfloat16 [2, 16, 4, 16, 2048], P('dp', 'row', None, None, 'col'), may hold values from -2 to 2
Outputs:
- block_output: bfloat16 [2, 16, 4, 16, 2048], P('dp', 'row', None, None, 'col')
- input_grad: bfloat16 [2, 16, 4, 16, 2048], P('dp', 'row', None, None, 'col')
- up_grad: bfloat16 [2048, 4096], P(('dp', 'row'), 'col')
- down_grad: bfloat16 [2048, 4096], P(('dp', 'row'), 'col')
- kernel_grad: float32 [125, 4096], P(None, 'col')
All inputs are finite; a program needn't handle non-finite values.
Results may differ from a plain program's by a relative error of at most 0.012.
Values may be sent and summed in bfloat16 or wider, within the bound.
A program may use at most 128 MiB of HBM per device.

v0:
```python
import jax
import jax.numpy as jnp
from jax import lax
from jax.sharding import PartitionSpec as P


def with_halo(shard, sides, width):
    for axis, dim in sides:
        peers, length = (lax.axis_size(axis), shard.shape[dim])
        up = [(i, (i + 1) % peers) for i in range(peers - 1)]
        down = [(j, i) for i, j in up]
        last = lax.slice_in_dim(shard, length - width, length, axis=dim)
        initial = lax.slice_in_dim(shard, 0, width, axis=dim)
        before = lax.ppermute(last, axis, up)
        after = lax.ppermute(initial, axis, down)
        shard = jnp.concatenate([before, shard, after], axis=dim)
    return shard


def depth_margin(field):
    extended = with_halo(field, (("row", 1),), 2)
    return jnp.pad(extended, ((0, 0), (0, 0), (2, 2), (2, 2), (0, 0)))


def stencil_sum(padded, kernel, mirror):
    planes = padded.shape[1] - 4
    tile_x = padded.shape[2] - 4
    tile_y = padded.shape[3] - 4
    result = jnp.zeros(padded.shape[:1] + (planes, tile_x, tile_y, padded.shape[4]), jnp.float32)
    for depth_step in range(5):
        for row_step in range(5):
            for col_step in range(5):
                first_z = depth_step + mirror * (4 - 2 * depth_step)
                first_x = row_step + mirror * (4 - 2 * row_step)
                first_y = col_step + mirror * (4 - 2 * col_step)
                window = padded[
                    :,
                    first_z : first_z + planes,
                    first_x : first_x + tile_x,
                    first_y : first_y + tile_y,
                    :,
                ]
                result = result + kernel[25 * depth_step + 5 * row_step + col_step] * window
    return result


def kernel_terms(padded, grad_field):
    planes = grad_field.shape[1]
    tile_x = grad_field.shape[2]
    tile_y = grad_field.shape[3]
    grad_wide = grad_field.astype(jnp.float32)
    rows_list = []
    for depth_step in range(5):
        for row_step in range(5):
            for col_step in range(5):
                window = padded[
                    :,
                    depth_step : depth_step + planes,
                    row_step : row_step + tile_x,
                    col_step : col_step + tile_y,
                    :,
                ]
                rows_list.append(jnp.sum(window * grad_wide, axis=(0, 1, 2, 3)))
    return jnp.stack(rows_list)


def column_sum(partial_value, field_shape):
    return lax.psum_scatter(
        partial_value.reshape(field_shape).astype(jnp.bfloat16),
        "col",
        scatter_dimension=4,
        tiled=True,
    ).astype(jnp.float32)


def spread_product(left_rows, right_rows):
    return lax.dot_general(
        left_rows, right_rows, (((0,), (0,)), ((), ())), preferred_element_type=jnp.float32
    )


def on_device(inputs, up_weight, down_weight, kernel, cotangent):
    states, planes, tile_x, tile_y, local_width = inputs.shape
    voxels = states * planes * tile_x * tile_y
    local_hidden = up_weight.shape[1]
    contract_last = (((1,), (1,)), ((), ()))
    input_rows, cotangent_rows = (
        lax.all_gather(inputs, "col", axis=4, tiled=True),
        lax.all_gather(cotangent, "col", axis=4, tiled=True),
    )
    full_width = input_rows.shape[4]
    field_shape = (states, planes, tile_x, tile_y, full_width)
    hidden_shape = (states, planes, tile_x, tile_y, local_hidden)
    flat_inputs = input_rows.reshape(voxels, full_width)
    hidden = jnp.dot(flat_inputs, up_weight, preferred_element_type=jnp.float32).astype(
        jnp.bfloat16
    )
    hidden_pad = depth_margin(hidden.reshape(hidden_shape))
    preact = stencil_sum(hidden_pad, kernel, 0)
    activation = jax.nn.silu(preact).astype(jnp.bfloat16)
    flat_act = activation.reshape(voxels, local_hidden)
    mixed_share = column_sum(
        lax.dot_general(flat_act, down_weight, contract_last, preferred_element_type=jnp.float32),
        field_shape,
    )
    block_output = (inputs.astype(jnp.float32) + mixed_share).astype(jnp.bfloat16)
    flat_cotangent = cotangent_rows.reshape(voxels, full_width)
    act_grad = jnp.dot(flat_cotangent, down_weight, preferred_element_type=jnp.float32).reshape(
        hidden_shape
    )
    logistic = jax.nn.sigmoid(preact)
    preact_grad = (act_grad * logistic * (1.0 + preact * (1.0 - logistic))).astype(jnp.bfloat16)
    grad_pad = depth_margin(preact_grad)
    hidden_grad = stencil_sum(grad_pad, kernel, 1).astype(jnp.bfloat16)
    kernel_grad = lax.psum(
        kernel_terms(hidden_pad, preact_grad).astype(jnp.bfloat16), ("dp", "row")
    ).astype(jnp.float32)
    flat_grad_hidden = hidden_grad.reshape(voxels, local_hidden)
    input_share = column_sum(
        lax.dot_general(
            flat_grad_hidden, up_weight, contract_last, preferred_element_type=jnp.float32
        ),
        field_shape,
    )
    input_grad = (cotangent.astype(jnp.float32) + input_share).astype(jnp.bfloat16)
    both_share = lax.psum_scatter(
        jnp.concatenate(
            [
                spread_product(flat_inputs, flat_grad_hidden),
                spread_product(flat_cotangent, flat_act),
            ],
            axis=1,
        ).astype(jnp.bfloat16),
        ("dp", "row"),
        scatter_dimension=0,
        tiled=True,
    ).astype(jnp.float32)
    up_share = both_share[:, :local_hidden]
    down_share = both_share[:, local_hidden:]
    up_grad = up_share.astype(jnp.bfloat16)
    down_grad = down_share.astype(jnp.bfloat16)
    return (block_output, input_grad, up_grad, down_grad, kernel_grad)


def solution(mesh):
    placed = (
        P("dp", "row", None, None, "col"),
        P(None, "col"),
        P(None, "col"),
        P(None, "col"),
        P("dp", "row", None, None, "col"),
    )
    return jax.shard_map(
        on_device,
        mesh=mesh,
        in_specs=placed,
        out_specs=(
            P("dp", "row", None, None, "col"),
            P("dp", "row", None, None, "col"),
            P(("dp", "row"), "col"),
            P(("dp", "row"), "col"),
            P(None, "col"),
        ),
        check_vma=False,
    )
```

profile of v0, /device:TPU:0, one launch (start us, length us, event | category | flops | bytes accessed | tf_op | source)
XLA Modules:
  0.0 385.0 jit_solution(17823461748566457241)
XLA Ops:
  7.9 0.7 all-gather.5.cloned.1.call-update
  8.7 1.3 fusion.328
  10.0 2.0 fusion.327
  12.0 1.9 fusion.326
  13.9 1.9 fusion.325
  15.9 2.0 fusion.324
  17.9 22.3 %all-gather.3.cloned.1.call-done = bf16[1,4,4,16,2048]{4,3,2,1,0:T(8,128)(2,1)} async-done(((bf16[1,4,4,16,512]{4,3,2,1,0:T(8,128)(2,1)}), bf16[1,4,4,16,2048]{4,3,2,1,0:T(8,128)(2,1)}) %all-gather.3.cloned.1.call-update) | async-done | bytes 1048592 | tf_op jit(solution)/shard_map/all_gather | solution.py:88
  40.2 3.8 convolution_convert_fusion
  44.5 1.3 collective-permute-start.1
  45.8 4.7 %collective-permute-start = (bf16[1,2,4,16,1024]{4,3,2,1,0:T(8,128)(2,1)S(1)}, bf16[1,2,4,16,1024]{4,3,2,1,0:T(8,128)(2,1)S(1)}, u32[]{:S(2)}, u32[]{:S(2)}) collective-permute-start(bf16[1,2,4,16,1024]{4,3,2,1,0:T(8,128)(2,1)S(1)} %get-tuple-element.142), channel_id=1, source_target_pairs={{0,4},{4,8},{8,12},{1,5},{5,9},{9,13},{2,6},{6,10},{10,14},{3,7},{... | collective-permute-start | bytes 786440 | tf_op jit(solution)/shard_map/ppermute | solution.py:14
  50.5 1.1 fusion.330
  51.7 1.4 fusion.329
  53.3 2.3 collective-permute-done.1
  55.6 0.8 select_maximum_fusion.2
  57.1 28.9 %fusion.159 = f32[1,4,4,16,1024]{4,3,2,1,0:T(8,128)} fusion(bf16[1,4,4,16,1024]{4,3,2,1,0:T(8,128)(2,1)S(1)} %bitcast.210, f32[1024]{0:T(1024)S(1)} %bitcast.420, f32[1024]{0:T(1024)S(1)} %bitcast.422, f32[1024]{0:T(1024)} %bitcast.366, f32[1024]{0:T(1024)} %bitcast.368, f32[1024]{0:T(1024)} %bitcast.370, f32[1024]{0:T(1024)} %bitcast.372, ...), kind=kLoop, calls=%fused_computation.406 | loop fusion | flops 99090432 | bytes 65523712 | tf_op jit(solution)/shard_map/add | solution.py:43
  86.1 6.9 %fusion.303 = (bf16[1024]{0:T(1024)(128)(2,1)}, bf16[1024]{0:T(1024)(128)(2,1)}, bf16[1024]{0:T(1024)(128)(2,1)}, bf16[1024]{0:T(1024)(128)(2,1)}, bf16[1024]{0:...) fusion(bf16[1,8,8,20,1024]{4,3,2,1,0:T(8,128)(2,1)S(1)} %select, ...), kind=kOutput, calls=%fused_computation.550 | convolution fusion | flops 1086573568 | bytes 13658112 | tf_op jit(solution)/shard_map/dot_general | solution.py:108
  93.1 3.4 fusion.308
  96.5 3.4 fusion.309
  99.9 3.4 fusion.306
  103.3 3.4 fusion.304
  106.7 3.3 fusion.305
  110.0 3.4 fusion.307
  113.8 2.3 fusion.21
  116.0 0.8 stack.622
  129.2 0.7 stack.531
  132.6 0.7 stack.536
  156.6 0.7 stack.572
  157.3 0.7 stack.573
  164.0 0.7 stack.600
  168.1 0.7 stack.606
  175.0 10.6 %stack.629 = bf16[125,1024]{1,0:T(8,128)(2,1)} concatenate(bf16[1,1024]{1,0:T(2,128)(2,1)S(1)} %stack.504, bf16[1,1024]{1,0:T(2,128)(2,1)S(1)} %stack.505, bf16[1,1024]{1,0:T(2,128)(2,1)S(1)} %stack.506, bf16[1,1024]{1,0:T(2,128)(2,1)S(1)} %stack.507, bf16[1,1024]{1,0:T(2,128)(2,1)S(1)} %stack.508, bf16[1,1024]{1,0:T(2,128)(2,1)S(1)} %stack.509, bf16[1,1024]{1,0:T(2,128)(2,1)S(1)} %stack.510, ...), dimensions={0} | concatenate | bytes 512000 | tf_op jit(solution)/shard_map/stack | solution.py:64
  185.7 1.3 collective-permute-start.3
  187.0 6.4 %collective-permute-start.2 = (bf16[1,2,4,16,1024]{4,3,2,1,0:T(8,128)(2,1)S(1)}, bf16[1,2,4,16,1024]{4,3,2,1,0:T(8,128)(2,1)S(1)}, u32[]{:S(2)}, u32[]{:S(2)}) collective-permute-start(bf16[1,2,4,16,1024]{4,3,2,1,0:T(8,128)(2,1)S(1)} %get-tuple-element.140), channel_id=1, source_target_pairs={{0,4},{4,8},{8,12},{1,5},{5,9},{9,13},{2,6},{6,10},{10,14},{3,7},{... | collective-permute-start | bytes 786440 | tf_op jit(solution)/shard_map/ppermute | solution.py:14
  193.5 4.5 %fusion.10 = bf16[2048,1024]{0,1:T(8,128)(2,1)} fusion(bf16[1,4,4,16,2048]{4,3,2,1,0:T(8,128)(2,1)} %all-gather.5.cloned.1.call-done, f32[1,4,4,16,1024]{4,3,2,1,0:T(8,128)S(1)} %copy-done.7), kind=kOutput, calls=%fused_computation.143 | convolution fusion | flops 1077149696 | bytes 6291456 | tf_op jit(solution)/shard_map/dot_general | solution.py:77
  198.5 1.1 select_maximum_fusion
  200.0 30.2 %add_convert_fusion = bf16[1,4,4,16,1024]{4,3,2,1,0:T(8,128)(2,1)S(1)} fusion(bf16[1,4,4,16,1024]{4,3,2,1,0:T(8,128)(2,1)S(1)} %copy-done.1, bf16[1,2,4,16,1024]{4,3,2,1,0:T(8,128)(2,1)S(1)} %collective-permute-done.2, bf16[1,2,4,16,1024]{4,3,2,1,0:T(8,128)(2,1)S(1)} %collective-permute-done.3, bf16[1,8,8,20,1024]{4,3,2,1,0:T(8,128)(2,1)S(1)} %select_maximum_fusion, ...), kind=kLoop, calls=%fused_computation.560 | loop fusion | flops 99352576 | bytes 64999424 | tf_op jit(solution)/shard_map/convert_element_type | solution.py:114
  230.2 4.5 %fusion.18 = bf16[1,4,4,16,2048]{4,3,2,1,0:T(8,128)(2,1)} fusion(bf16[2048,1024]{1,0:T(8,128)(2,1)} %param.6, bf16[1,4,4,16,1024]{4,3,2,1,0:T(8,128)(2,1)S(1)} %add_convert_fusion), kind=kOutput, calls=%fused_computation.151 | convolution fusion | flops 1074266112 | bytes 5767168 | tf_op jit(solution)/shard_map/dot_general | solution.py:120
  234.8 4.5 %fusion.9 = bf16[2048,1024]{0,1:T(8,128)(2,1)} fusion(bf16[1,4,4,16,2048]{4,3,2,1,0:T(8,128)(2,1)} %all-gather.3.cloned.1.call-done, bf16[1,4,4,16,1024]{4,3,2,1,0:T(8,128)(2,1)S(1)} %add_convert_fusion), kind=kOutput, calls=%fused_computation.142 | convolution fusion | flops 1075838976 | bytes 5767168 | tf_op jit(solution)/shard_map/dot_general | solution.py:77
  239.3 8.4 %pad_maximum_fusion = bf16[2048,2048]{0,1:T(8,128)(2,1)} fusion(bf16[2048,1024]{0,1:T(8,128)(2,1)} %fusion.10, bf16[2048,1024]{0,1:T(8,128)(2,1)} %fusion.9), kind=kLoop, calls=%fused_computation.130 | loop fusion | flops 16777216 | bytes 16777216 | tf_op jit(solution)/shard_map/concatenate | solution.py:127
  247.7 1.8 convert_element_type.1202
  249.6 23.6 %reduce-scatter.4.cloned.1.call-done = bf16[1,4,4,16,512]{4,3,2,1,0:T(8,128)(2,1)} async-done(((bf16[1,4,4,16,2048]{4,3,2,1,0:T(8,128)(2,1)}), bf16[1,4,4,16,512]{4,3,2,1,0:T(8,128)(2,1)}) %reduce-scatter.4.cloned.1.call-update) | async-done | bytes 262160 | tf_op jit(solution)/shard_map/reduce_scatter | solution.py:68
  273.2 1.7 add_convert_fusion.2
  274.9 26.2 %reduce-scatter.6.cloned.1.call-done = bf16[1,4,4,16,512]{4,3,2,1,0:T(8,128)(2,1)} async-done(((bf16[1,4,4,16,2048]{4,3,2,1,0:T(8,128)(2,1)}), bf16[1,4,4,16,512]{4,3,2,1,0:T(8,128)(2,1)}) %reduce-scatter.6.cloned.1.call-update) | async-done | bytes 262160 | tf_op jit(solution)/shard_map/reduce_scatter | solution.py:68
  301.1 1.7 add_convert_fusion.1
  302.9 71.9 %reduce-scatter.8.cloned.1.call-done = bf16[256,2048]{0,1:T(8,128)(2,1)} async-done(((bf16[2048,2048]{0,1:T(8,128)(2,1)}), bf16[256,2048]{0,1:T(8,128)(2,1)}) %reduce-scatter.8.cloned.1.call-update) | async-done | bytes 1048592 | tf_op jit(solution)/shard_map/reduce_scatter | solution.py:126
  374.8 1.3 fusion.321
  376.1 1.0 copy.11
  377.1 1.0 copy.10
  (449 shorter events, 55.1 us)
Async XLA Ops:
  7.2 33.1 %all-gather.3.cloned.1.call-start = ((), (), s32[]{:S(2)}) async-start(), calls=%async_computation.3 | async-start | bytes 1310720 | tf_op jit(solution)/shard_map/all_gather | solution.py:88
  7.9 78.2 %all-gather.5.cloned.1.call-start = ((), (), s32[]{:S(2)}) async-start(), calls=%async_computation.5 | async-start | bytes 1310720 | tf_op jit(solution)/shard_map/all_gather | solution.py:89
  8.6 239.1 %all-reduce.4.cloned.1.call-start = ((), (), s32[]{:S(2)}) async-start(), calls=%async_computation.8 | async-start | bytes 524288 | tf_op jit(solution)/shard_map/psum | solution.py:115
  44.5 11.1 %collective-permute-start.1 = (bf16[1,2,4,16,1024]{4,3,2,1,0:T(8,128)(2,1)S(1)}, bf16[1,2,4,16,1024]{4,3,2,1,0:T(8,128)(2,1)S(1)}, u32[]{:S(2)}, u32[]{:S(2)}) collective-permute-start(bf16[1,2,4,16,1024]{4,3,2,1,0:T(8,128)(2,1)S(1)} %get-tuple-element.141), channel_id=1, source_target_pairs={{4,0},{8,4},{12,8},{5,1},{9,5},{13,9},{6,2},{10,6},{14,10},{7,3},{... | collective-permute-start | bytes 786440 | tf_op jit(solution)/shard_map/ppermute | solution.py:15
  45.8 9.8 %collective-permute-start = (bf16[1,2,4,16,1024]{4,3,2,1,0:T(8,128)(2,1)S(1)}, bf16[1,2,4,16,1024]{4,3,2,1,0:T(8,128)(2,1)S(1)}, u32[]{:S(2)}, u32[]{:S(2)}) collective-permute-start(bf16[1,2,4,16,1024]{4,3,2,1,0:T(8,128)(2,1)S(1)} %get-tuple-element.142), channel_id=1, source_target_pairs={{0,4},{4,8},{8,12},{1,5},{5,9},{9,13},{2,6},{6,10},{10,14},{3,7},{... | collective-permute-start | bytes 786440 | tf_op jit(solution)/shard_map/ppermute | solution.py:14
  113.4 60.1 %copy-start.154 = (bf16[1024]{0:T(1024)(128)(2,1)S(1)}, bf16[1024]{0:T(1024)(128)(2,1)}, u32[]{:S(2)}) copy-start(bf16[1024]{0:T(1024)(128)(2,1)} %get-tuple-element.82) | copy-start | bytes 6148
  113.4 60.8 %copy-start.153 = (bf16[1024]{0:T(1024)(128)(2,1)S(1)}, bf16[1024]{0:T(1024)(128)(2,1)}, u32[]{:S(2)}) copy-start(bf16[1024]{0:T(1024)(128)(2,1)} %get-tuple-element.83) | copy-start | bytes 6148
  113.4 60.8 %copy-start.152 = (bf16[1024]{0:T(1024)(128)(2,1)S(1)}, bf16[1024]{0:T(1024)(128)(2,1)}, u32[]{:S(2)}) copy-start(bf16[1024]{0:T(1024)(128)(2,1)} %get-tuple-element.84) | copy-start | bytes 6148
  113.4 60.8 %copy-start.151 = (bf16[1024]{0:T(1024)(128)(2,1)S(1)}, bf16[1024]{0:T(1024)(128)(2,1)}, u32[]{:S(2)}) copy-start(bf16[1024]{0:T(1024)(128)(2,1)} %get-tuple-element.85) | copy-start | bytes 6148
  113.5 60.8 %copy-start.150 = (bf16[1024]{0:T(1024)(128)(2,1)S(1)}, bf16[1024]{0:T(1024)(128)(2,1)}, u32[]{:S(2)}) copy-start(bf16[1024]{0:T(1024)(128)(2,1)} %get-tuple-element.86) | copy-start | bytes 6148
  113.5 60.8 %copy-start.149 = (bf16[1024]{0:T(1024)(128)(2,1)S(1)}, bf16[1024]{0:T(1024)(128)(2,1)}, u32[]{:S(2)}) copy-start(bf16[1024]{0:T(1024)(128)(2,1)} %get-tuple-element.87) | copy-start | bytes 6148
  113.5 60.8 %copy-start.148 = (bf16[1024]{0:T(1024)(128)(2,1)S(1)}, bf16[1024]{0:T(1024)(128)(2,1)}, u32[]{:S(2)}) copy-start(bf16[1024]{0:T(1024)(128)(2,1)} %get-tuple-element.88) | copy-start | bytes 6148
  113.5 60.9 %copy-start.147 = (bf16[1024]{0:T(1024)(128)(2,1)S(1)}, bf16[1024]{0:T(1024)(128)(2,1)}, u32[]{:S(2)}) copy-start(bf16[1024]{0:T(1024)(128)(2,1)} %get-tuple-element.89) | copy-start | bytes 6148
  113.5 60.9 %copy-start.146 = (bf16[1024]{0:T(1024)(128)(2,1)S(1)}, bf16[1024]{0:T(1024)(128)(2,1)}, u32[]{:S(2)}) copy-start(bf16[1024]{0:T(1024)(128)(2,1)} %get-tuple-element.90) | copy-start | bytes 6148
  113.5 60.9 %copy-start.145 = (bf16[1024]{0:T(1024)(128)(2,1)S(1)}, bf16[1024]{0:T(1024)(128)(2,1)}, u32[]{:S(2)}) copy-start(bf16[1024]{0:T(1024)(128)(2,1)} %get-tuple-element.91) | copy-start | bytes 6148
  113.5 60.9 %copy-start.144 = (bf16[1024]{0:T(1024)(128)(2,1)S(1)}, bf16[1024]{0:T(1024)(128)(2,1)}, u32[]{:S(2)}) copy-start(bf16[1024]{0:T(1024)(128)(2,1)} %get-tuple-element.92) | copy-start | bytes 6148
  113.5 60.9 %copy-start.143 = (bf16[1024]{0:T(1024)(128)(2,1)S(1)}, bf16[1024]{0:T(1024)(128)(2,1)}, u32[]{:S(2)}) copy-start(bf16[1024]{0:T(1024)(128)(2,1)} %get-tuple-element.93) | copy-start | bytes 6148
  113.5 60.9 %copy-start.142 = (bf16[1024]{0:T(1024)(128)(2,1)S(1)}, bf16[1024]{0:T(1024)(128)(2,1)}, u32[]{:S(2)}) copy-start(bf16[1024]{0:T(1024)(128)(2,1)} %get-tuple-element.94) | copy-start | bytes 6148
  113.5 60.9 %copy-start.141 = (bf16[1024]{0:T(1024)(128)(2,1)S(1)}, bf16[1024]{0:T(1024)(128)(2,1)}, u32[]{:S(2)}) copy-start(bf16[1024]{0:T(1024)(128)(2,1)} %get-tuple-element.95) | copy-start | bytes 6148
  113.5 60.9 %copy-start.140 = (bf16[1024]{0:T(1024)(128)(2,1)S(1)}, bf16[1024]{0:T(1024)(128)(2,1)}, u32[]{:S(2)}) copy-start(bf16[1024]{0:T(1024)(128)(2,1)} %get-tuple-element.96) | copy-start | bytes 6148
  113.6 61.0 %copy-start.139 = (bf16[1024]{0:T(1024)(128)(2,1)S(1)}, bf16[1024]{0:T(1024)(128)(2,1)}, u32[]{:S(2)}) copy-start(bf16[1024]{0:T(1024)(128)(2,1)} %get-tuple-element.97) | copy-start | bytes 6148
  113.6 61.0 %copy-start.138 = (bf16[1024]{0:T(1024)(128)(2,1)S(1)}, bf16[1024]{0:T(1024)(128)(2,1)}, u32[]{:S(2)}) copy-start(bf16[1024]{0:T(1024)(128)(2,1)} %get-tuple-element.98) | copy-start | bytes 6148
  113.6 61.0 %copy-start.136 = (bf16[1024]{0:T(1024)(128)(2,1)S(1)}, bf16[1024]{0:T(1024)(128)(2,1)}, u32[]{:S(2)}) copy-start(bf16[1024]{0:T(1024)(128)(2,1)} %get-tuple-element.99) | copy-start | bytes 6148
  113.6 61.0 %copy-start.137 = (bf16[1024]{0:T(1024)(128)(2,1)S(1)}, bf16[1024]{0:T(1024)(128)(2,1)}, u32[]{:S(2)}) copy-start(bf16[1024]{0:T(1024)(128)(2,1)} %get-tuple-element.47) | copy-start | bytes 6148
  113.6 61.0 %copy-start.135 = (bf16[1024]{0:T(1024)(128)(2,1)S(1)}, bf16[1024]{0:T(1024)(128)(2,1)}, u32[]{:S(2)}) copy-start(bf16[1024]{0:T(1024)(128)(2,1)} %get-tuple-element.48) | copy-start | bytes 6148
  113.6 61.0 %copy-start.134 = (bf16[1024]{0:T(1024)(128)(2,1)S(1)}, bf16[1024]{0:T(1024)(128)(2,1)}, u32[]{:S(2)}) copy-start(bf16[1024]{0:T(1024)(128)(2,1)} %get-tuple-element.49) | copy-start | bytes 6148
  113.6 61.0 %copy-start.133 = (bf16[1024]{0:T(1024)(128)(2,1)S(1)}, bf16[1024]{0:T(1024)(128)(2,1)}, u32[]{:S(2)}) copy-start(bf16[1024]{0:T(1024)(128)(2,1)} %get-tuple-element.50) | copy-start | bytes 6148
  113.6 61.0 %copy-start.132 = (bf16[1024]{0:T(1024)(128)(2,1)S(1)}, bf16[1024]{0:T(1024)(128)(2,1)}, u32[]{:S(2)}) copy-start(bf16[1024]{0:T(1024)(128)(2,1)} %get-tuple-element.51) | copy-start | bytes 6148
  113.6 61.1 %copy-start.131 = (bf16[1024]{0:T(1024)(128)(2,1)S(1)}, bf16[1024]{0:T(1024)(128)(2,1)}, u32[]{:S(2)}) copy-start(bf16[1024]{0:T(1024)(128)(2,1)} %get-tuple-element.52) | copy-start | bytes 6148
  113.7 61.1 %copy-start.130 = (bf16[1024]{0:T(1024)(128)(2,1)S(1)}, bf16[1024]{0:T(1024)(128)(2,1)}, u32[]{:S(2)}) copy-start(bf16[1024]{0:T(1024)(128)(2,1)} %get-tuple-element.53) | copy-start | bytes 6148
  113.7 61.1 %copy-start.129 = (bf16[1024]{0:T(1024)(128)(2,1)S(1)}, bf16[1024]{0:T(1024)(128)(2,1)}, u32[]{:S(2)}) copy-start(bf16[1024]{0:T(1024)(128)(2,1)} %get-tuple-element.54) | copy-start | bytes 6148
  113.7 61.1 %copy-start.128 = (bf16[1024]{0:T(1024)(128)(2,1)S(1)}, bf16[1024]{0:T(1024)(128)(2,1)}, u32[]{:S(2)}) copy-start(bf16[1024]{0:T(1024)(128)(2,1)} %get-tuple-element.55) | copy-start | bytes 6148
  113.7 61.1 %copy-start.127 = (bf16[1024]{0:T(1024)(128)(2,1)S(1)}, bf16[1024]{0:T(1024)(128)(2,1)}, u32[]{:S(2)}) copy-start(bf16[1024]{0:T(1024)(128)(2,1)} %get-tuple-element.56) | copy-start | bytes 6148
  113.7 61.1 %copy-start.126 = (bf16[1024]{0:T(1024)(128)(2,1)S(1)}, bf16[1024]{0:T(1024)(128)(2,1)}, u32[]{:S(2)}) copy-start(bf16[1024]{0:T(1024)(128)(2,1)} %get-tuple-element.57) | copy-start | bytes 6148
  113.7 61.1 %copy-start.125 = (bf16[1024]{0:T(1024)(128)(2,1)S(1)}, bf16[1024]{0:T(1024)(128)(2,1)}, u32[]{:S(2)}) copy-start(bf16[1024]{0:T(1024)(128)(2,1)} %get-tuple-element.58) | copy-start | bytes 6148
  113.7 61.2 %copy-start.124 = (bf16[1024]{0:T(1024)(128)(2,1)S(1)}, bf16[1024]{0:T(1024)(128)(2,1)}, u32[]{:S(2)}) copy-start(bf16[1024]{0:T(1024)(128)(2,1)} %get-tuple-element.59) | copy-start | bytes 6148
  113.7 61.2 %copy-start.123 = (bf16[1024]{0:T(1024)(128)(2,1)S(1)}, bf16[1024]{0:T(1024)(128)(2,1)}, u32[]{:S(2)}) copy-start(bf16[1024]{0:T(1024)(128)(2,1)} %get-tuple-element.60) | copy-start | bytes 6148
  113.7 61.2 %copy-start.122 = (bf16[1024]{0:T(1024)(128)(2,1)S(1)}, bf16[1024]{0:T(1024)(128)(2,1)}, u32[]{:S(2)}) copy-start(bf16[1024]{0:T(1024)(128)(2,1)} %get-tuple-element.61) | copy-start | bytes 6148
  113.7 61.2 %copy-start.121 = (bf16[1024]{0:T(1024)(128)(2,1)S(1)}, bf16[1024]{0:T(1024)(128)(2,1)}, u32[]{:S(2)}) copy-start(bf16[1024]{0:T(1024)(128)(2,1)} %get-tuple-element.62) | copy-start | bytes 6148
  113.8 61.2 %copy-start.120 = (bf16[1024]{0:T(1024)(128)(2,1)S(1)}, bf16[1024]{0:T(1024)(128)(2,1)}, u32[]{:S(2)}) copy-start(bf16[1024]{0:T(1024)(128)(2,1)} %get-tuple-element.63) | copy-start | bytes 6148
  116.0 77.5 %copy-start.7 = (f32[1,4,4,16,1024]{4,3,2,1,0:T(8,128)S(1)}, f32[1,4,4,16,1024]{4,3,2,1,0:T(8,128)}, u32[]{:S(2)}) copy-start(f32[1,4,4,16,1024]{4,3,2,1,0:T(8,128)} %fusion.159) | copy-start | bytes 3145732
  185.6 87.5 %reduce-scatter.4.cloned.1.call-start = ((), (), s32[]{:S(2)}) async-start(), calls=%async_computation.4 | async-start | bytes 1310720 | tf_op jit(solution)/shard_map/reduce_scatter | solution.py:68
  185.7 12.7 %collective-permute-start.3 = (bf16[1,2,4,16,1024]{4,3,2,1,0:T(8,128)(2,1)S(1)}, bf16[1,2,4,16,1024]{4,3,2,1,0:T(8,128)(2,1)S(1)}, u32[]{:S(2)}, u32[]{:S(2)}) collective-permute-start(bf16[1,2,4,16,1024]{4,3,2,1,0:T(8,128)(2,1)S(1)} %get-tuple-element.139), channel_id=1, source_target_pairs={{4,0},{8,4},{12,8},{5,1},{9,5},{13,9},{6,2},{10,6},{14,10},{7,3},{... | collective-permute-start | bytes 786440 | tf_op jit(solution)/shard_map/ppermute | solution.py:15
  187.0 11.4 %collective-permute-start.2 = (bf16[1,2,4,16,1024]{4,3,2,1,0:T(8,128)(2,1)S(1)}, bf16[1,2,4,16,1024]{4,3,2,1,0:T(8,128)(2,1)S(1)}, u32[]{:S(2)}, u32[]{:S(2)}) collective-permute-start(bf16[1,2,4,16,1024]{4,3,2,1,0:T(8,128)(2,1)S(1)} %get-tuple-element.140), channel_id=1, source_target_pairs={{0,4},{4,8},{8,12},{1,5},{5,9},{9,13},{2,6},{6,10},{10,14},{3,7},{... | collective-permute-start | bytes 786440 | tf_op jit(solution)/shard_map/ppermute | solution.py:14
  193.5 107.7 %reduce-scatter.6.cloned.1.call-start = ((), (), s32[]{:S(2)}) async-start(), calls=%async_computation.6 | async-start | bytes 1310720 | tf_op jit(solution)/shard_map/reduce_scatter | solution.py:68
  234.8 140.0 %reduce-scatter.8.cloned.1.call-start = ((), (), s32[]{:S(2)}) async-start(), calls=%async_computation.7 | async-start | bytes 9437184 | tf_op jit(solution)/shard_map/reduce_scatter | solution.py:126
  247.7 25.5 %copy-start.8 = (bf16[1,4,4,16,512]{4,3,2,1,0:T(8,128)(2,1)S(1)}, bf16[1,4,4,16,512]{4,3,2,1,0:T(8,128)(2,1)}, u32[]{:S(2)}) copy-start(bf16[1,4,4,16,512]{4,3,2,1,0:T(8,128)(2,1)} %param.5) | copy-start | bytes 786436
  247.7 53.5 %copy-start.9 = (bf16[1,4,4,16,512]{4,3,2,1,0:T(8,128)(2,1)S(1)}, bf16[1,4,4,16,512]{4,3,2,1,0:T(8,128)(2,1)}, u32[]{:S(2)}) copy-start(bf16[1,4,4,16,512]{4,3,2,1,0:T(8,128)(2,1)} %param.9) | copy-start | bytes 786436
  (118 other events, 737.3 us)
Sparse Core Ops, SparseCore 0:
  9.6 30.6 all-gather.2
  41.8 27.4 all-gather.4
  185.8 58.5 all-reduce.3
  246.6 26.5 reduce-scatter.3
  275.3 25.7 reduce-scatter.5
  304.9 69.9 reduce-scatter.7
where the time goes:
time: 388 us; the launch traced here: 385 us
  waiting for transfers between devices  148 us (38%)
  other arithmetic  95.6 us (25%)
  local copies, waits for them, and re-layouts  84.1 us (22%)
  matrix products  26.5 us (7%)
  between operations  16.9 us (4%)
  starting transfers between devices  14 us (4%)
    reduce_scatter x1, waiting for transfers between devices, on_device(): lax.psum_scatter(jnp.concatenate([spread_product(flat_inputs, flat_grad_h...  71.9 us
    another operation x126, local copies, waits for them, and re-layouts, kernel_terms(): return jnp.stack(rows_list)  68.4 us
    reduce_scatter x2, waiting for transfers between devices, column_sum(): lax.psum_scatter(partial_value.reshape(field_shape).astype(jnp.bfloat16),...  49.8 us
    convert_element_type x1, other arithmetic, on_device(): hidden_grad = stencil_sum(grad_pad, kernel, 1).astype(jnp.bfloat16)  30.2 us
    add x1, other arithmetic, stencil_sum(): result = result + kernel[25 * depth_step + 5 * row_step + col_step] * window  28.9 us
    all_gather x1, waiting for transfers between devices, on_device(): lax.all_gather(inputs, 'col', axis=4, tiled=True)  22.3 us
    reduce_sum x7, other arithmetic, kernel_terms(): rows_list.append(jnp.sum(window * grad_wide, axis=(0, 1, 2, 3)))  20.7 us
    slice x7, local copies, waits for them, and re-layouts, stencil_sum(): result = result + kernel[25 * depth_step + 5 * row_step + col_step] * window  11.7 us
  transfers between devices with their start and end apart: 10, of which 5 were waited for; matrix products, arithmetic and copies ran while one was open for 27% of the time, Pallas kernels for 0%

commit v1 on v0

--- a/solution.py
+++ b/solution.py
@@ -2,6 +2,19 @@
 import jax.numpy as jnp
 from jax import lax
 from jax.sharding import PartitionSpec as P
+
+
+def ring_gather(array, axis, dim):
+    ways = lax.axis_size(axis)
+    up = [(d, (d + 1) % ways) for d in range(ways)]
+    down = [(d, (d - 1) % ways) for d in range(ways)]
+    earlier, later = ([array], [array])
+    for _ in range(ways // 2):
+        earlier.append(lax.ppermute(earlier[-1], axis, up))
+    for _ in range((ways - 1) // 2):
+        later.append(lax.ppermute(later[-1], axis, down))
+    line = jnp.concatenate([*earlier[::-1], *later[1:]], axis=dim)
+    return jnp.roll(line, (lax.axis_index(axis) - ways // 2) * array.shape[dim], axis=dim)
 
 
 def with_halo(shard, sides, width):
@@ -85,7 +98,7 @@
     local_hidden = up_weight.shape[1]
     contract_last = (((1,), (1,)), ((), ()))
     input_rows, cotangent_rows = (
-        lax.all_gather(inputs, "col", axis=4, tiled=True),
+        ring_gather(inputs, "col", 4),
         lax.all_gather(cotangent, "col", axis=4, tiled=True),
     )
     full_width = input_rows.shape[4]

time: 388 us -> 322 us (0.83)
  local copies, waits for them, and re-layouts: 84.1 us -> 28.1 us
  waiting for transfers between devices: 148 us -> 142 us
    another operation x126, local copies, waits for them, and re-layouts: 68.4 us -> 11.3 us  [kernel_terms(): return jnp.stack(rows_list)]
    all_gather x1 -> x0, waiting for transfers between devices: 22.3 us -> none  [on_device(): lax.all_gather(inputs, 'col', axis=4, tiled=True)]
    ppermute x0 -> x3, waiting for transfers between devices: none -> 15.6 us  [the longest x2 15.6 us: ring_gather(): earlier.append(lax.ppermute(earlier[-1], axis, up))]
    ppermute x0 -> x3, starting transfers between devices: none -> 5.17 us  [the longest x2 3.08 us: ring_gather(): earlier.append(lax.ppermute(earlier[-1], axis, up))]
  transfers between devices with their start and end apart: 10 -> 12, of which waited for: 5 -> 6; matrix products, arithmetic and copies ran while one was open for 27% -> 33% of each run, Pallas kernels for 0% -> 0%
where the time goes in v1:
time: 322 us; the launch traced here: 321 us
  waiting for transfers between devices  142 us (44%)
  other arithmetic  91.9 us (29%)
  local copies, waits for them, and re-layouts  28.1 us (9%)
  matrix products  24.4 us (8%)
  starting transfers between devices  17.7 us (5%)
  between operations  17 us (5%)
    reduce_scatter x1, waiting for transfers between devices, on_device(): lax.psum_scatter(jnp.concatenate([spread_product(flat_inputs, flat_grad_h...  71.9 us
    reduce_scatter x2, waiting for transfers between devices, column_sum(): lax.psum_scatter(partial_value.reshape(field_shape).astype(jnp.bfloat16),...  52.3 us
    convert_element_type x1, other arithmetic, on_device(): hidden_grad = stencil_sum(grad_pad, kernel, 1).astype(jnp.bfloat16)  30.2 us
    add x1, other arithmetic, stencil_sum(): result = result + kernel[25 * depth_step + 5 * row_step + col_step] * window  28.8 us
    reduce_sum x7, other arithmetic, kernel_terms(): rows_list.append(jnp.sum(window * grad_wide, axis=(0, 1, 2, 3)))  17.2 us
    ppermute x2, waiting for transfers between devices, ring_gather(): earlier.append(lax.ppermute(earlier[-1], axis, up))  15.6 us
    slice x7, local copies, waits for them, and re-layouts, stencil_sum(): result = result + kernel[25 * depth_step + 5 * row_step + col_step] * window  11.7 us
    another operation x126, local copies, waits for them, and re-layouts, kernel_terms(): return jnp.stack(rows_list)  11.3 us
  transfers between devices with their start and end apart: 12, of which 6 were waited for; matrix products, arithmetic and copies ran while one was open for 33% of the time, Pallas kernels for 0%

profile of v1, /device:TPU:0, one launch (start us, length us, event | category | flops | bytes accessed | tf_op | source)
XLA Modules:
  0.0 320.7 jit_solution(7414247959728036554)
XLA Ops:
  7.2 3.1 collective-permute-start
  10.3 2.1 collective-permute-start.2
  12.5 1.3 fusion.327
  13.8 2.0 fusion.326
  15.8 1.9 fusion.325
  17.7 2.0 collective-permute-done
  19.7 1.9 fusion.324
  21.7 1.4 fusion.323
  23.3 13.6 %collective-permute-done.1 = bf16[1,4,4,16,512]{4,3,2,1,0:T(8,128)(2,1)S(1)} collective-permute-done((bf16[1,4,4,16,512]{4,3,2,1,0:T(8,128)(2,1)S(1)}, bf16[1,4,4,16,512]{4,3,2,1,0:T(8,128)(2,1)S(1)}, u32[]{:S(2)}, u32[]{:S(2)}) %collective-permute-start.1) | collective-permute-done | bytes 262176 | tf_op jit(solution)/shard_map/ppermute | solution.py:13
  37.0 1.0 constant_dynamic-update-slice_fusion.5
  38.1 0.1 constant_dynamic-slice_fusion
  38.2 1.3 convolution_convert_fusion
  40.0 1.3 collective-permute-start.4
  41.3 4.7 %collective-permute-start.3 = (bf16[1,2,4,16,1024]{4,3,2,1,0:T(8,128)(2,1)S(1)}, bf16[1,2,4,16,1024]{4,3,2,1,0:T(8,128)(2,1)S(1)}, u32[]{:S(2)}, u32[]{:S(2)}) collective-permute-start(bf16[1,2,4,16,1024]{4,3,2,1,0:T(8,128)(2,1)S(1)} %get-tuple-element.142), channel_id=1, source_target_pairs={{0,4},{4,8},{8,12},{1,5},{5,9},{9,13},{2,6},{6,10},{10,14},{3,7},{... | collective-permute-start | bytes 786440 | tf_op jit(solution)/shard_map/ppermute | solution.py:27
  46.0 1.1 fusion.329
  47.2 2.0 fusion.328
  49.3 1.6 collective-permute-done.4
  51.0 0.8 select_maximum_fusion.2
  52.6 28.8 %fusion.158 = f32[1,4,4,16,1024]{4,3,2,1,0:T(8,128)} fusion(bf16[1,4,4,16,1024]{4,3,2,1,0:T(8,128)(2,1)S(1)} %bitcast.206, f32[1024]{0:T(1024)S(1)} %bitcast.417, f32[1024]{0:T(1024)S(1)} %bitcast.419, f32[1024]{0:T(1024)S(1)} %bitcast.363, f32[1024]{0:T(1024)S(1)} %bitcast.365, f32[1024]{0:T(1024)S(1)} %bitcast.367, f32[1024]{0:T(1024)S(1)} %bitcast.369, ...), kind=kLoop, calls=%fused_computation.405 | loop fusion | flops 99090432 | bytes 65523712 | tf_op jit(solution)/shard_map/add | solution.py:56
  81.4 6.3 %fusion.302 = (bf16[1024]{0:T(1024)(128)(2,1)S(1)}, bf16[1024]{0:T(1024)(128)(2,1)S(1)}, bf16[1024]{0:T(1024)(128)(2,1)S(1)}, bf16[1024]{0:T(1024)(128)(2,1)S(1)...) fusion(bf16[1,8,8,20,1024]{4,3,2,1,0:T(8,128)(2,1)S(1)} %select, ...), kind=kOutput, calls=%fused_computation.549 | convolution fusion | flops 1086573568 | bytes 13658112 | tf_op jit(solution)/shard_map/dot_general | solution.py:121
  87.8 2.8 fusion.307
  90.5 2.8 fusion.308
  93.4 3.0 fusion.305
  96.4 2.8 fusion.303
  99.2 2.6 fusion.304
  101.8 2.8 fusion.306
  104.7 0.4 fusion.296
  106.7 10.6 %stack.629 = bf16[125,1024]{1,0:T(8,128)(2,1)} concatenate(bf16[1,1024]{1,0:T(2,128)(2,1)S(1)} %stack.504, bf16[1,1024]{1,0:T(2,128)(2,1)S(1)} %stack.505, bf16[1,1024]{1,0:T(2,128)(2,1)S(1)} %stack.506, bf16[1,1024]{1,0:T(2,128)(2,1)S(1)} %stack.507, bf16[1,1024]{1,0:T(2,128)(2,1)S(1)} %stack.508, bf16[1,1024]{1,0:T(2,128)(2,1)S(1)} %stack.509, bf16[1,1024]{1,0:T(2,128)(2,1)S(1)} %stack.510, ...), dimensions={0} | concatenate | bytes 512000 | tf_op jit(solution)/shard_map/stack | solution.py:77
  117.4 1.3 collective-permute-start.6
  118.8 5.0 %collective-permute-start.5 = (bf16[1,2,4,16,1024]{4,3,2,1,0:T(8,128)(2,1)S(1)}, bf16[1,2,4,16,1024]{4,3,2,1,0:T(8,128)(2,1)S(1)}, u32[]{:S(2)}, u32[]{:S(2)}) collective-permute-start(bf16[1,2,4,16,1024]{4,3,2,1,0:T(8,128)(2,1)S(1)} %get-tuple-element.140), channel_id=1, source_target_pairs={{0,4},{4,8},{8,12},{1,5},{5,9},{9,13},{2,6},{6,10},{10,14},{3,7},{... | collective-permute-start | bytes 786440 | tf_op jit(solution)/shard_map/ppermute | solution.py:27
  123.8 4.5 %fusion.20 = bf16[1,4,4,16,2048]{4,3,2,1,0:T(8,128)(2,1)} fusion(bf16[2048,1024]{1,0:T(8,128)(2,1)} %param.7, f32[1,4,4,16,1024]{4,3,2,1,0:T(8,128)S(1)} %copy-done.10), kind=kOutput, calls=%fused_computation.151 | convolution fusion | flops 1075576832 | bytes 6291456 | tf_op jit(solution)/shard_map/dot_general | solution.py:116
  128.7 0.0 reduce-scatter.6.cloned.1.call-start
  128.7 1.1 select_maximum_fusion
  130.3 30.2 %add_convert_fusion = bf16[1,4,4,16,1024]{4,3,2,1,0:T(8,128)(2,1)S(1)} fusion(bf16[1,4,4,16,1024]{4,3,2,1,0:T(8,128)(2,1)S(1)} %copy-done.1, bf16[1,2,4,16,1024]{4,3,2,1,0:T(8,128)(2,1)S(1)} %collective-permute-done.5, bf16[1,2,4,16,1024]{4,3,2,1,0:T(8,128)(2,1)S(1)} %collective-permute-done.6, bf16[1,8,8,20,1024]{4,3,2,1,0:T(8,128)(2,1)S(1)} %select_maximum_fusion, ...), kind=kLoop, calls=%fused_computation.559 | loop fusion | flops 99352576 | bytes 64999424 | tf_op jit(solution)/shard_map/convert_element_type | solution.py:127
  160.5 4.5 %fusion.17 = bf16[1,4,4,16,2048]{4,3,2,1,0:T(8,128)(2,1)} fusion(bf16[2048,1024]{1,0:T(8,128)(2,1)} %param.6, bf16[1,4,4,16,1024]{4,3,2,1,0:T(8,128)(2,1)S(1)} %add_convert_fusion), kind=kOutput, calls=%fused_computation.150 | convolution fusion | flops 1074266112 | bytes 5767168 | tf_op jit(solution)/shard_map/dot_general | solution.py:133
  165.0 0.0 reduce-scatter.8.cloned.1.call-start
  165.1 4.6 %fusion.9 = bf16[2048,1024]{0,1:T(8,128)(2,1)} fusion(bf16[1,4,4,16,2048]{4,3,2,1,0:T(8,128)(2,1)} %all-gather.2.cloned.1.call-done, f32[1,4,4,16,1024]{4,3,2,1,0:T(8,128)S(1)} %copy-done.10), kind=kOutput, calls=%fused_computation.142 | convolution fusion | flops 1077149696 | bytes 6291456 | tf_op jit(solution)/shard_map/dot_general | solution.py:90
  169.7 3.3 %bitcast_convert_fusion.1 = bf16[2048,1024]{0,1:T(8,128)(2,1)} fusion(bf16[1,4,4,16,2048]{4,3,2,1,0:T(8,128)(2,1)S(1)} %copy-done.5, bf16[1,4,4,16,1024]{4,3,2,1,0:T(8,128)(2,1)S(1)} %add_convert_fusion), kind=kOutput, calls=%fused_computation.132 | convolution fusion | flops 1075838976 | bytes 5767168 | tf_op jit(solution)/shard_map/dot_general | solution.py:90
  173.0 8.4 %pad_maximum_fusion = bf16[2048,2048]{0,1:T(8,128)(2,1)} fusion(bf16[2048,1024]{0,1:T(8,128)(2,1)} %fusion.9, bf16[2048,1024]{0,1:T(8,128)(2,1)} %bitcast_convert_fusion.1), kind=kLoop, calls=%fused_computation.130 | loop fusion | flops 16777216 | bytes 16777216 | tf_op jit(solution)/shard_map/concatenate | solution.py:140
  181.4 1.8 convert_element_type.1202
  183.2 26.0 %reduce-scatter.4.cloned.1.call-done = bf16[1,4,4,16,512]{4,3,2,1,0:T(8,128)(2,1)} async-done(((bf16[1,4,4,16,2048]{4,3,2,1,0:T(8,128)(2,1)}), bf16[1,4,4,16,512]{4,3,2,1,0:T(8,128)(2,1)}) %reduce-scatter.4.cloned.1.call-update) | async-done | bytes 262160 | tf_op jit(solution)/shard_map/reduce_scatter | solution.py:81
  209.2 1.7 add_convert_fusion.2
  211.0 26.3 %reduce-scatter.6.cloned.1.call-done = bf16[1,4,4,16,512]{4,3,2,1,0:T(8,128)(2,1)} async-done(((bf16[1,4,4,16,2048]{4,3,2,1,0:T(8,128)(2,1)}), bf16[1,4,4,16,512]{4,3,2,1,0:T(8,128)(2,1)}) %reduce-scatter.6.cloned.1.call-update) | async-done | bytes 262160 | tf_op jit(solution)/shard_map/reduce_scatter | solution.py:81
  237.3 1.7 add_convert_fusion.1
  239.0 71.9 %reduce-scatter.8.cloned.1.call-done = bf16[256,2048]{0,1:T(8,128)(2,1)} async-done(((bf16[2048,2048]{0,1:T(8,128)(2,1)}), bf16[256,2048]{0,1:T(8,128)(2,1)}) %reduce-scatter.8.cloned.1.call-update) | async-done | bytes 1048592 | tf_op jit(solution)/shard_map/reduce_scatter | solution.py:139
  310.9 1.3 fusion.320
  312.2 1.0 copy.11
  313.2 1.0 copy.10
  (407 shorter events, 1.7 us)
Async XLA Ops:
  7.2 30.9 %copy-start.8 = (bf16[1,4,4,16,512]{4,3,2,1,0:T(8,128)(2,1)S(1)}, bf16[1,4,4,16,512]{4,3,2,1,0:T(8,128)(2,1)}, u32[]{:S(2)}) copy-start(bf16[1,4,4,16,512]{4,3,2,1,0:T(8,128)(2,1)} %param.5) | copy-start | bytes 786436
  7.2 74.2 %all-gather.2.cloned.1.call-start = ((), (), s32[]{:S(2)}) async-start(), calls=%async_computation.4 | async-start | bytes 1310720 | tf_op jit(solution)/shard_map/all_gather | solution.py:102
  7.2 12.5 %collective-permute-start = (bf16[1,4,4,16,512]{4,3,2,1,0:T(8,128)(2,1)}, bf16[1,4,4,16,512]{4,3,2,1,0:T(8,128)(2,1)S(1)}, u32[]{:S(2)}, u32[]{:S(2)}) collective-permute-start(bf16[1,4,4,16,512]{4,3,2,1,0:T(8,128)(2,1)} %param.5), channel_id=1, source_target_pairs={{0,1},{1,2},{2,3},{3,0},{4,5},{5,6},{6,7},{7,4},{8,9},{9,10},{10,1... | collective-permute-start | bytes 786440 | tf_op jit(solution)/shard_map/ppermute | solution.py:13
  10.3 27.6 %collective-permute-start.2 = (bf16[1,4,4,16,512]{4,3,2,1,0:T(8,128)(2,1)}, bf16[1,4,4,16,512]{4,3,2,1,0:T(8,128)(2,1)S(1)}, u32[]{:S(2)}, u32[]{:S(2)}) collective-permute-start(bf16[1,4,4,16,512]{4,3,2,1,0:T(8,128)(2,1)} %param.5), channel_id=1, source_target_pairs={{0,3},{1,0},{2,1},{3,2},{4,7},{5,4},{6,5},{7,6},{8,11},{9,8},{10,9... | collective-permute-start | bytes 786440 | tf_op jit(solution)/shard_map/ppermute | solution.py:15
  12.4 169.0 %all-reduce.4.cloned.1.call-start = ((), (), s32[]{:S(2)}) async-start(), calls=%async_computation.7 | async-start | bytes 524288 | tf_op jit(solution)/shard_map/psum | solution.py:128
  19.7 17.2 %collective-permute-start.1 = (bf16[1,4,4,16,512]{4,3,2,1,0:T(8,128)(2,1)S(1)}, bf16[1,4,4,16,512]{4,3,2,1,0:T(8,128)(2,1)S(1)}, u32[]{:S(2)}, u32[]{:S(2)}) collective-permute-start(bf16[1,4,4,16,512]{4,3,2,1,0:T(8,128)(2,1)S(1)} %collective-permute-done), channel_id=1, source_target_pairs={{0,1},{1,2},{2,3},{3,0},{4,5},{5,6},{6,7},{7,4},{8,9},{9,10},{10,1... | collective-permute-start | bytes 786440 | tf_op jit(solution)/shard_map/ppermute | solution.py:13
  23.1 28.7 %copy-start.91 = (f32[1,1024]{1,0:T(1,128)}, f32[1,1024]{1,0:T(1,128)S(1)}, u32[]{:S(2)}) copy-start(f32[1,1024]{1,0:T(1,128)S(1)} %get-tuple-element.143) | copy-start | bytes 12292
  23.1 28.7 %copy-start.92 = (f32[1,1024]{1,0:T(1,128)}, f32[1,1024]{1,0:T(1,128)S(1)}, u32[]{:S(2)}) copy-start(f32[1,1024]{1,0:T(1,128)S(1)} %get-tuple-element.144) | copy-start | bytes 12292
  23.1 28.7 %copy-start.93 = (f32[1,1024]{1,0:T(1,128)}, f32[1,1024]{1,0:T(1,128)S(1)}, u32[]{:S(2)}) copy-start(f32[1,1024]{1,0:T(1,128)S(1)} %get-tuple-element.145) | copy-start | bytes 12292
  23.1 28.7 %copy-start.94 = (f32[1,1024]{1,0:T(1,128)}, f32[1,1024]{1,0:T(1,128)S(1)}, u32[]{:S(2)}) copy-start(f32[1,1024]{1,0:T(1,128)S(1)} %get-tuple-element.146) | copy-start | bytes 12292
  23.1 28.7 %copy-start.95 = (f32[1,1024]{1,0:T(1,128)}, f32[1,1024]{1,0:T(1,128)S(1)}, u32[]{:S(2)}) copy-start(f32[1,1024]{1,0:T(1,128)S(1)} %get-tuple-element.147) | copy-start | bytes 12292
  23.2 28.7 %copy-start.96 = (f32[1,1024]{1,0:T(1,128)}, f32[1,1024]{1,0:T(1,128)S(1)}, u32[]{:S(2)}) copy-start(f32[1,1024]{1,0:T(1,128)S(1)} %get-tuple-element.148) | copy-start | bytes 12292
  23.2 28.7 %copy-start.97 = (f32[1,1024]{1,0:T(1,128)}, f32[1,1024]{1,0:T(1,128)S(1)}, u32[]{:S(2)}) copy-start(f32[1,1024]{1,0:T(1,128)S(1)} %get-tuple-element.149) | copy-start | bytes 12292
  23.2 28.7 %copy-start.98 = (f32[1,1024]{1,0:T(1,128)}, f32[1,1024]{1,0:T(1,128)S(1)}, u32[]{:S(2)}) copy-start(f32[1,1024]{1,0:T(1,128)S(1)} %get-tuple-element.150) | copy-start | bytes 12292
  23.2 28.7 %copy-start.99 = (f32[1,1024]{1,0:T(1,128)}, f32[1,1024]{1,0:T(1,128)S(1)}, u32[]{:S(2)}) copy-start(f32[1,1024]{1,0:T(1,128)S(1)} %get-tuple-element.151) | copy-start | bytes 12292
  23.2 28.7 %copy-start.100 = (f32[1,1024]{1,0:T(1,128)}, f32[1,1024]{1,0:T(1,128)S(1)}, u32[]{:S(2)}) copy-start(f32[1,1024]{1,0:T(1,128)S(1)} %get-tuple-element.152) | copy-start | bytes 12292
  23.2 28.7 %copy-start.101 = (f32[1,1024]{1,0:T(1,128)}, f32[1,1024]{1,0:T(1,128)S(1)}, u32[]{:S(2)}) copy-start(f32[1,1024]{1,0:T(1,128)S(1)} %get-tuple-element.153) | copy-start | bytes 12292
  23.2 28.7 %copy-start.102 = (f32[1,1024]{1,0:T(1,128)}, f32[1,1024]{1,0:T(1,128)S(1)}, u32[]{:S(2)}) copy-start(f32[1,1024]{1,0:T(1,128)S(1)} %get-tuple-element.154) | copy-start | bytes 12292
  23.2 28.7 %copy-start.103 = (f32[1,1024]{1,0:T(1,128)}, f32[1,1024]{1,0:T(1,128)S(1)}, u32[]{:S(2)}) copy-start(f32[1,1024]{1,0:T(1,128)S(1)} %get-tuple-element.155) | copy-start | bytes 12292
  23.2 28.7 %copy-start.104 = (f32[1,1024]{1,0:T(1,128)}, f32[1,1024]{1,0:T(1,128)S(1)}, u32[]{:S(2)}) copy-start(f32[1,1024]{1,0:T(1,128)S(1)} %get-tuple-element.156) | copy-start | bytes 12292
  23.2 28.7 %copy-start.105 = (f32[1,1024]{1,0:T(1,128)}, f32[1,1024]{1,0:T(1,128)S(1)}, u32[]{:S(2)}) copy-start(f32[1,1024]{1,0:T(1,128)S(1)} %get-tuple-element.157) | copy-start | bytes 12292
  23.3 28.7 %copy-start.106 = (f32[1,1024]{1,0:T(1,128)}, f32[1,1024]{1,0:T(1,128)S(1)}, u32[]{:S(2)}) copy-start(f32[1,1024]{1,0:T(1,128)S(1)} %get-tuple-element.158) | copy-start | bytes 12292
  23.3 28.7 %copy-start.107 = (f32[1,1024]{1,0:T(1,128)}, f32[1,1024]{1,0:T(1,128)S(1)}, u32[]{:S(2)}) copy-start(f32[1,1024]{1,0:T(1,128)S(1)} %get-tuple-element.159) | copy-start | bytes 12292
  23.3 28.7 %copy-start.108 = (f32[1,1024]{1,0:T(1,128)}, f32[1,1024]{1,0:T(1,128)S(1)}, u32[]{:S(2)}) copy-start(f32[1,1024]{1,0:T(1,128)S(1)} %get-tuple-element.160) | copy-start | bytes 12292
  23.3 28.7 %copy-start.109 = (f32[1,1024]{1,0:T(1,128)}, f32[1,1024]{1,0:T(1,128)S(1)}, u32[]{:S(2)}) copy-start(f32[1,1024]{1,0:T(1,128)S(1)} %get-tuple-element.161) | copy-start | bytes 12292
  23.3 14.9 %copy-start.128 = (bf16[2048,1024]{1,0:T(8,128)(2,1)S(1)}, bf16[2048,1024]{1,0:T(8,128)(2,1)}, u32[]{:S(2)}) copy-start(bf16[2048,1024]{1,0:T(8,128)(2,1)} %param.6) | copy-start | bytes 12582916
  39.5 12.7 %copy-start.12 = (f32[1,1024]{1,0:T(1,128)S(1)}, f32[1,1024]{1,0:T(1,128)}, u32[]{:S(2)}) copy-start(f32[1,1024]{1,0:T(1,128)} %get-tuple-element.217) | copy-start | bytes 12292
  39.5 12.7 %copy-start.14 = (f32[1,1024]{1,0:T(1,128)S(1)}, f32[1,1024]{1,0:T(1,128)}, u32[]{:S(2)}) copy-start(f32[1,1024]{1,0:T(1,128)} %get-tuple-element.218) | copy-start | bytes 12292
  39.6 12.7 %copy-start.16 = (f32[1,1024]{1,0:T(1,128)S(1)}, f32[1,1024]{1,0:T(1,128)}, u32[]{:S(2)}) copy-start(f32[1,1024]{1,0:T(1,128)} %get-tuple-element.181) | copy-start | bytes 12292
  39.6 12.7 %copy-start.18 = (f32[1,1024]{1,0:T(1,128)S(1)}, f32[1,1024]{1,0:T(1,128)}, u32[]{:S(2)}) copy-start(f32[1,1024]{1,0:T(1,128)} %get-tuple-element.182) | copy-start | bytes 12292
  39.6 12.7 %copy-start.20 = (f32[1,1024]{1,0:T(1,128)S(1)}, f32[1,1024]{1,0:T(1,128)}, u32[]{:S(2)}) copy-start(f32[1,1024]{1,0:T(1,128)} %get-tuple-element.183) | copy-start | bytes 12292
  39.6 12.7 %copy-start.22 = (f32[1,1024]{1,0:T(1,128)S(1)}, f32[1,1024]{1,0:T(1,128)}, u32[]{:S(2)}) copy-start(f32[1,1024]{1,0:T(1,128)} %get-tuple-element.184) | copy-start | bytes 12292
  39.6 12.7 %copy-start.24 = (f32[1,1024]{1,0:T(1,128)S(1)}, f32[1,1024]{1,0:T(1,128)}, u32[]{:S(2)}) copy-start(f32[1,1024]{1,0:T(1,128)} %get-tuple-element.185) | copy-start | bytes 12292
  39.6 12.7 %copy-start.26 = (f32[1,1024]{1,0:T(1,128)S(1)}, f32[1,1024]{1,0:T(1,128)}, u32[]{:S(2)}) copy-start(f32[1,1024]{1,0:T(1,128)} %get-tuple-element.186) | copy-start | bytes 12292
  39.6 12.7 %copy-start.28 = (f32[1,1024]{1,0:T(1,128)S(1)}, f32[1,1024]{1,0:T(1,128)}, u32[]{:S(2)}) copy-start(f32[1,1024]{1,0:T(1,128)} %get-tuple-element.187) | copy-start | bytes 12292
  39.6 12.7 %copy-start.30 = (f32[1,1024]{1,0:T(1,128)S(1)}, f32[1,1024]{1,0:T(1,128)}, u32[]{:S(2)}) copy-start(f32[1,1024]{1,0:T(1,128)} %get-tuple-element.188) | copy-start | bytes 12292
  39.6 12.7 %copy-start.32 = (f32[1,1024]{1,0:T(1,128)S(1)}, f32[1,1024]{1,0:T(1,128)}, u32[]{:S(2)}) copy-start(f32[1,1024]{1,0:T(1,128)} %get-tuple-element.189) | copy-start | bytes 12292
  40.0 11.0 %collective-permute-start.4 = (bf16[1,2,4,16,1024]{4,3,2,1,0:T(8,128)(2,1)S(1)}, bf16[1,2,4,16,1024]{4,3,2,1,0:T(8,128)(2,1)S(1)}, u32[]{:S(2)}, u32[]{:S(2)}) collective-permute-start(bf16[1,2,4,16,1024]{4,3,2,1,0:T(8,128)(2,1)S(1)} %get-tuple-element.141), channel_id=1, source_target_pairs={{4,0},{8,4},{12,8},{5,1},{9,5},{13,9},{6,2},{10,6},{14,10},{7,3},{... | collective-permute-start | bytes 786440 | tf_op jit(solution)/shard_map/ppermute | solution.py:28
  41.3 9.7 %collective-permute-start.3 = (bf16[1,2,4,16,1024]{4,3,2,1,0:T(8,128)(2,1)S(1)}, bf16[1,2,4,16,1024]{4,3,2,1,0:T(8,128)(2,1)S(1)}, u32[]{:S(2)}, u32[]{:S(2)}) collective-permute-start(bf16[1,2,4,16,1024]{4,3,2,1,0:T(8,128)(2,1)S(1)} %get-tuple-element.142), channel_id=1, source_target_pairs={{0,4},{4,8},{8,12},{1,5},{5,9},{9,13},{2,6},{6,10},{10,14},{3,7},{... | collective-permute-start | bytes 786440 | tf_op jit(solution)/shard_map/ppermute | solution.py:27
  87.7 16.9 %copy-start = (bf16[1,4,4,16,1024]{4,3,2,1,0:T(8,128)(2,1)}, bf16[1,4,4,16,1024]{4,3,2,1,0:T(8,128)(2,1)S(1)}, u32[]{:S(2)}) copy-start(bf16[1,4,4,16,1024]{4,3,2,1,0:T(8,128)(2,1)S(1)} %get-tuple-element.268) | copy-start | bytes 1572868
  104.6 19.2 %copy-start.10 = (f32[1,4,4,16,1024]{4,3,2,1,0:T(8,128)S(1)}, f32[1,4,4,16,1024]{4,3,2,1,0:T(8,128)}, u32[]{:S(2)}) copy-start(f32[1,4,4,16,1024]{4,3,2,1,0:T(8,128)} %fusion.158) | copy-start | bytes 3145732
  117.4 91.9 %reduce-scatter.4.cloned.1.call-start = ((), (), s32[]{:S(2)}) async-start(), calls=%async_computation.3 | async-start | bytes 1310720 | tf_op jit(solution)/shard_map/reduce_scatter | solution.py:81
  117.4 11.3 %collective-permute-start.6 = (bf16[1,2,4,16,1024]{4,3,2,1,0:T(8,128)(2,1)S(1)}, bf16[1,2,4,16,1024]{4,3,2,1,0:T(8,128)(2,1)S(1)}, u32[]{:S(2)}, u32[]{:S(2)}) collective-permute-start(bf16[1,2,4,16,1024]{4,3,2,1,0:T(8,128)(2,1)S(1)} %get-tuple-element.139), channel_id=1, source_target_pairs={{4,0},{8,4},{12,8},{5,1},{9,5},{13,9},{6,2},{10,6},{14,10},{7,3},{... | collective-permute-start | bytes 786440 | tf_op jit(solution)/shard_map/ppermute | solution.py:28
  118.8 10.0 %collective-permute-start.5 = (bf16[1,2,4,16,1024]{4,3,2,1,0:T(8,128)(2,1)S(1)}, bf16[1,2,4,16,1024]{4,3,2,1,0:T(8,128)(2,1)S(1)}, u32[]{:S(2)}, u32[]{:S(2)}) collective-permute-start(bf16[1,2,4,16,1024]{4,3,2,1,0:T(8,128)(2,1)S(1)} %get-tuple-element.140), channel_id=1, source_target_pairs={{0,4},{4,8},{8,12},{1,5},{5,9},{9,13},{2,6},{6,10},{10,14},{3,7},{... | collective-permute-start | bytes 786440 | tf_op jit(solution)/shard_map/ppermute | solution.py:27
  128.7 108.6 %reduce-scatter.6.cloned.1.call-start = ((), (), s32[]{:S(2)}) async-start(), calls=%async_computation.5 | async-start | bytes 1310720 | tf_op jit(solution)/shard_map/reduce_scatter | solution.py:81
  165.0 145.9 %reduce-scatter.8.cloned.1.call-start = ((), (), s32[]{:S(2)}) async-start(), calls=%async_computation.6 | async-start | bytes 9437184 | tf_op jit(solution)/shard_map/reduce_scatter | solution.py:139
  181.3 27.9 %copy-start.9 = (bf16[1,4,4,16,512]{4,3,2,1,0:T(8,128)(2,1)S(1)}, bf16[1,4,4,16,512]{4,3,2,1,0:T(8,128)(2,1)}, u32[]{:S(2)}) copy-start(bf16[1,4,4,16,512]{4,3,2,1,0:T(8,128)(2,1)} %param.5) | copy-start | bytes 786436
  181.3 55.9 %copy-start.11 = (bf16[1,4,4,16,512]{4,3,2,1,0:T(8,128)(2,1)S(1)}, bf16[1,4,4,16,512]{4,3,2,1,0:T(8,128)(2,1)}, u32[]{:S(2)}) copy-start(bf16[1,4,4,16,512]{4,3,2,1,0:T(8,128)(2,1)} %param.9) | copy-start | bytes 786436
  (93 other events, 539.6 us)
Sparse Core Ops, SparseCore 0:
  12.5 34.7 all-gather.1
  117.5 62.7 all-reduce.3
  182.7 26.5 reduce-scatter.3
  211.4 25.8 reduce-scatter.5
  241.0 69.9 reduce-scatter.7
